TPU v7x, 256 devices: a whole 4x4x8 slice. The times are simulated.
256 devices in a mesh: gx: 16 (over x, y), gy: 2 (over core), gz: 8 (over z).
Axes of the slice: x: 4, y: 4, z: 8, core: 2. Of those that a mesh axis runs over, the one named last changes fastest.
Arguments:
- field: float32 [2, 1024, 128, 1024], P(None, 'gx', 'gy', 'gz'), as said below
- start_basis: float32 [1024, 256], replicated, may hold values from -6 to 6
Outputs:
- factor: float32 [1024, 256], P('gx')
- core: float32 [2, 256, 128, 1024], P(None, 'gx', 'gy', 'gz')
Inputs may be any that keep to these rules, and one draw needn't show every extreme that they name: Real-valued field; no structure is promised.
All inputs are finite; a program needn't handle non-finite values.
Results may differ from a plain program's by a relative error of at most 0.0002.
Values sent between devices are 32-bit elements; how exact they have to be, the bound alone decides.
A program may use at most 64 MiB of HBM per device.

v0:
```python
import jax
import jax.numpy as jnp
from jax import lax
from jax.sharding import PartitionSpec as P

ITERS = 2


def orthonormal(image):
    small = jnp.dot(image.T, image, precision=lax.Precision.HIGHEST)
    lower = jnp.linalg.cholesky(small)
    return jax.scipy.linalg.solve_triangular(lower, image.T, lower=True).T


def per_device(field, start_basis):
    comps, slab, cells_y, cells_z = field.shape
    flat_field = field.reshape(comps, slab, cells_y * cells_z)
    fibers = lax.all_to_all(flat_field, "gx", split_axis=2, concat_axis=1, tiled=True)
    basis = start_basis
    local_gram = jnp.einsum("crm,csm->rs", fibers, fibers, precision=lax.Precision.HIGHEST)
    gram = lax.psum(local_gram, ("gx", "gy", "gz"))
    for step in range(ITERS):
        image = jnp.dot(gram, basis, precision=lax.Precision.HIGHEST)
        basis = orthonormal(image)
    projected = jnp.einsum("rk,crm->ckm", basis, fibers, precision=lax.Precision.HIGHEST)
    returned = lax.all_to_all(projected, "gx", split_axis=1, concat_axis=2, tiled=True)
    offset = lax.axis_index("gx") * slab
    factor = lax.dynamic_slice_in_dim(basis, offset, slab, 0)
    return (factor, returned.reshape(comps, returned.shape[1], cells_y, cells_z))


def solution(mesh):
    placed = (P(None, "gx", "gy", "gz"), P())
    return jax.shard_map(
        per_device,
        mesh=mesh,
        in_specs=placed,
        out_specs=(P("gx", None), P(None, "gx", "gy", "gz")),
        check_vma=False,
    )
```

profile of v0, /device:TPU:97, one launch (start us, length us, event | category | flops | bytes accessed | tf_op | source)
XLA Modules:
  0.0 604.0 jit_solution(12621777568615691695)
XLA Ops:
  7.2 0.0 copy-start
  7.2 0.0 all-reduce.3.cloned.1.call-start
  7.2 8.4 %copy.13 = f32[2,64,64,128]{1,0,3,2:T(2,128)} copy(f32[2,64,64,128]{3,2,1,0:T(8,128)} %param.5) | data formatting | bytes 8388608 | tf_op args[0]
  15.7 15.1 %reshape.52 = f32[16,1,65536]{2,1,0:T(1,128)} reshape(f32[8192,2,64]{2,1,0:T(2,128)} %bitcast.97) | data formatting | bytes 8388608
  30.8 56.1 %all_to_all.33 = f32[16,1,65536]{2,1,0:T(1,128)} all-to-all(f32[16,1,65536]{2,1,0:T(1,128)} %reshape.52), channel_id=1, replica_groups=mesh['gx'=16,'gy'=2,'gz'=8] {'gx'}, dimensions={0} | all-to-all | bytes 8388608 | tf_op jit(solution)/shard_map/all_to_all | solution.py:18
  86.8 0.5 broadcast.87
  87.3 13.7 %reduce.8 = f32[16,65536]{1,0:T(8,128)} reduce(f32[16,1,65536]{2,1,0:T(1,128)} %all_to_all.33, f32[]{:T(128)} %broadcast.87), dimensions={1}, to_apply=%all_to_all.24.reduce_sub_computation | reduce | bytes 8388612 | tf_op jit(solution)/shard_map/all_to_all | solution.py:18
  101.0 9.7 %reshape.53 = f32[8192,2,64]{2,1,0:T(2,128)} reshape(f32[16,65536]{1,0:T(8,128)} %reduce.8) | data formatting | bytes 8388608
  110.7 12.2 %copy.26 = f32[2,64,16,512]{3,1,2,0:T(8,128)} copy(f32[2,64,16,512]{1,0,3,2:T(2,128)} %bitcast.96) | data formatting | bytes 8388608 | tf_op jit(solution)/shard_map/all_to_all | solution.py:18
  122.9 17.6 %convolution_bitcast_fusion = f32[1024,1024]{1,0:T(8,128)} fusion(f32[2,1024,512]{2,1,0:T(8,128)} %bitcast.98), kind=kOutput, calls=%fused_computation.4 | convolution fusion | flops 12884901888 | bytes 8388608 | tf_op jit(solution)/shard_map/crm,csm->rs/dot_general | solution.py:20
  140.6 0.0 all-reduce.3.cloned.1.call-update
  140.6 270.4 %all-reduce.3.cloned.1.call-done = f32[1024,1024]{1,0:T(8,128)} async-done(((f32[1024,1024]{1,0:T(8,128)}), f32[1024,1024]{1,0:T(8,128)}) %all-reduce.3.cloned.1.call-update) | async-done | bytes 4194320 | tf_op jit(solution)/shard_map/psum | solution.py:21
  411.0 0.0 copy-done
  411.0 5.5 fusion.32
  416.5 1.8 fusion.33
  418.3 0.1 copy.16
  418.5 11.7 %cholesky.130 = f32[128,128]{1,0:T(8,128)S(1)} custom-call(f32[128,128]{1,0:T(8,128)S(1)} %cholesky.194), custom_call_target="Cholesky" | custom-call | tf_op jit(solution)/shard_map/jit(cholesky)/cholesky | solution.py:11
  430.3 9.8 %custom-call.13 = f32[1,128,128]{1,2,0:T(8,128)S(1)} custom-call(f32[1,128,128]{2,1,0:T(8,128)S(1)} %get-tuple-element.53), custom_call_target="InvertDiagBlocksLowerTriangular" | custom-call | tf_op jit(solution)/shard_map/jit(cholesky)/cholesky | solution.py:11
  440.1 0.2 constant_dynamic-update-slice_fusion.3
  440.3 0.3 convolution_subtract_fusion.3
  440.6 11.7 %cholesky.147 = f32[128,128]{1,0:T(8,128)S(1)} custom-call(f32[128,128]{1,0:T(8,128)S(1)} %convolution_subtract_fusion.3), custom_call_target="Cholesky" | custom-call | tf_op jit(solution)/shard_map/jit(cholesky)/cholesky | solution.py:11
  452.3 0.7 compare_reduce_fusion.2
  467.1 0.1 triangular_solve.75
  467.2 3.9 while.4
  467.2 0.6 fusion.55
  467.8 1.4 bitcast_dynamic-update-slice_fusion.4
  469.2 0.6 fusion.55
  469.8 1.4 bitcast_dynamic-update-slice_fusion.4
  471.2 19.7 %custom-call.14 = f32[2,128,128]{1,2,0:T(8,128)S(1)} custom-call(f32[2,128,128]{2,1,0:T(8,128)S(1)} %get-tuple-element.18), custom_call_target="InvertDiagBlocksLowerTriangular" | custom-call | tf_op jit(solution)/shard_map/jit(_solve_triangular)/triangular_solve | solution.py:12
  490.9 0.6 fusion.8
  491.5 1.0 convolution_subtract_fusion.1
  492.5 0.6 fusion.19
  493.2 5.3 fusion.2
  498.5 1.8 fusion.34
  500.3 0.1 copy.18
  500.5 11.7 %cholesky.164 = f32[128,128]{1,0:T(8,128)S(1)} custom-call(f32[128,128]{1,0:T(8,128)S(1)} %cholesky.197), custom_call_target="Cholesky" | custom-call | tf_op jit(solution)/shard_map/jit(cholesky)/cholesky | solution.py:11
  512.3 9.8 %custom-call.15 = f32[1,128,128]{1,2,0:T(8,128)S(1)} custom-call(f32[1,128,128]{2,1,0:T(8,128)S(1)} %get-tuple-element.49), custom_call_target="InvertDiagBlocksLowerTriangular" | custom-call | tf_op jit(solution)/shard_map/jit(cholesky)/cholesky | solution.py:11
  522.1 0.2 constant_dynamic-update-slice_fusion.1
  522.3 0.3 convolution_subtract_fusion.2
  522.6 11.7 %cholesky.181 = f32[128,128]{1,0:T(8,128)S(1)} custom-call(f32[128,128]{1,0:T(8,128)S(1)} %convolution_subtract_fusion.2), custom_call_target="Cholesky" | custom-call | tf_op jit(solution)/shard_map/jit(cholesky)/cholesky | solution.py:11
  534.3 0.6 compare_reduce_fusion
  535.0 0.6 compare_reduce_fusion.1
  536.9 0.2 select_select_fusion
  537.2 4.0 while.5
  537.2 0.6 fusion.56
  537.8 1.4 bitcast_dynamic-update-slice_fusion.5
  539.2 0.6 fusion.56
  539.8 1.4 bitcast_dynamic-update-slice_fusion.5
  541.2 19.7 %custom-call.16 = f32[2,128,128]{1,2,0:T(8,128)S(1)} custom-call(f32[2,128,128]{2,1,0:T(8,128)S(1)} %get-tuple-element.19), custom_call_target="InvertDiagBlocksLowerTriangular" | custom-call | tf_op jit(solution)/shard_map/jit(_solve_triangular)/triangular_solve | solution.py:12
  560.9 0.6 fusion.6
  561.5 1.0 convolution_subtract_fusion
  562.5 0.6 fusion.15
  563.2 5.7 convolution_bitcast_fusion.1
  568.9 1.8 copy.20
  570.7 4.6 all-to-all-start.1
  575.3 0.1 fusion.13
  575.4 0.7 copy.22
  576.1 17.8 %all-to-all-done.1 = f32[2,256,512]{2,0,1:T(2,128)} async-done(((f32[2,256,512]{2,0,1:T(2,128)}), f32[2,256,512]{2,0,1:T(2,128)}, u32[]{:S(2)}, u32[]{:S(2)}) %all-to-all-start.1) | async-done | bytes 1048608 | tf_op jit(solution)/shard_map/all_to_all | solution.py:26
  593.9 1.8 copy.21
  595.7 1.0 reshape.27
  (18 shorter events, 0.4 us)
Async XLA Ops:
  7.2 403.9 %copy-start = (f32[1024,256]{1,0:T(8,128)S(1)}, f32[1024,256]{1,0:T(8,128)}, u32[]{:S(2)}) copy-start(f32[1024,256]{1,0:T(8,128)} %param.6) | copy-start | bytes 3145732
  7.2 403.8 %all-reduce.3.cloned.1.call-start = ((), (), s32[]{:S(2)}) async-start(), calls=%async_computation.2 | async-start | bytes 8388608 | tf_op jit(solution)/shard_map/psum | solution.py:21
  570.7 23.2 %all-to-all-start.1 = ((f32[2,256,512]{2,0,1:T(2,128)}), f32[2,256,512]{2,0,1:T(2,128)}, u32[]{:S(2)}, u32[]{:S(2)}) async-start(f32[2,256,512]{2,0,1:T(2,128)} %copy.20), calls=%async_computation.1 | async-start | bytes 2097152 | tf_op jit(solution)/shard_map/all_to_all | solution.py:26
Sparse Core Ops, SparseCore 0:
  140.7 270.2 all-reduce.2
where the time goes:
time: 614 us; the launch traced here: 604 us
  waiting for transfers between devices  288 us (47%)
  other arithmetic  122 us (20%)
  local copies, waits for them, and re-layouts  59.5 us (10%)
  blocking collectives  56.1 us (9%)
  matrix products  43.3 us (7%)
  between operations  30.1 us (5%)
    psum x1, waiting for transfers between devices, per_device(): gram = lax.psum(local_gram, ('gx', 'gy', 'gz'))  270 us
    another operation x13, other arithmetic, orthonormal(): lower = jnp.linalg.cholesky(small)  68.5 us
    all_to_all x1, blocking collectives, per_device(): lax.all_to_all(flat_field, 'gx', split_axis=2, concat_axis=1, tiled=True)  56.1 us
    another operation x5, other arithmetic, orthonormal(): return jax.scipy.linalg.solve_triangular(lower, image.T, lower=True).T  39.6 us
    unnamed x6, local copies, waits for them, and re-layouts  33.9 us
    all_to_all x1, waiting for transfers between devices, per_device(): lax.all_to_all(projected, 'gx', split_axis=1, concat_axis=2, tiled=True)  17.8 us
    dot_general x1, matrix products, per_device(): jnp.einsum('crm,csm->rs', fibers, fibers, precision=lax.Precision.HIGHEST)  17.6 us
    all_to_all x1, other arithmetic, per_device(): lax.all_to_all(flat_field, 'gx', split_axis=2, concat_axis=1, tiled=True)  13.7 us
  transfers between devices with their start and end apart: 2, of which 2 were waited for; matrix products, arithmetic and copies ran while one was open for 0% of the time, Pallas kernels for 0%

commit v1 on v0

--- a/solution.py
+++ b/solution.py
@@ -18,7 +18,7 @@
     fibers = lax.all_to_all(flat_field, "gx", split_axis=2, concat_axis=1, tiled=True)
     basis = start_basis
     local_gram = jnp.einsum("crm,csm->rs", fibers, fibers, precision=lax.Precision.HIGHEST)
-    gram = lax.psum(local_gram, ("gx", "gy", "gz"))
+    gram = lax.psum(lax.psum(local_gram, ("gy", "gz")), "gx")
     for step in range(ITERS):
         image = jnp.dot(gram, basis, precision=lax.Precision.HIGHEST)
         basis = orthonormal(image)

time: 614 us -> 584 us (0.951)
  the two profiles are of different devices: /device:TPU:97 before, /device:TPU:32 now
where the time goes in v1:
time: 584 us; the launch traced here: 573 us
  waiting for transfers between devices  255 us (44%)
  other arithmetic  122 us (21%)
  local copies, waits for them, and re-layouts  59.5 us (10%)
  blocking collectives  57.9 us (10%)
  matrix products  43 us (7%)
  between operations  30.1 us (5%)
    psum x2, waiting for transfers between devices, per_device(): gram = lax.psum(lax.psum(local_gram, ('gy', 'gz')), 'gx')  238 us
    another operation x13, other arithmetic, orthonormal(): lower = jnp.linalg.cholesky(small)  68.5 us
    all_to_all x1, blocking collectives, per_device(): lax.all_to_all(flat_field, 'gx', split_axis=2, concat_axis=1, tiled=True)  57.9 us
    another operation x5, other arithmetic, orthonormal(): return jax.scipy.linalg.solve_triangular(lower, image.T, lower=True).T  39.6 us
    unnamed x6, local copies, waits for them, and re-layouts  33.9 us
    dot_general x1, matrix products, per_device(): jnp.einsum('crm,csm->rs', fibers, fibers, precision=lax.Precision.HIGHEST)  17.6 us
    all_to_all x1, waiting for transfers between devices, per_device(): lax.all_to_all(projected, 'gx', split_axis=1, concat_axis=2, tiled=True)  16.9 us
    all_to_all x1, other arithmetic, per_device(): lax.all_to_all(flat_field, 'gx', split_axis=2, concat_axis=1, tiled=True)  13.7 us
  transfers between devices with their start and end apart: 3, of which 3 were waited for; matrix products, arithmetic and copies ran while one was open for 0% of the time, Pallas kernels for 0%

profile of v1, /device:TPU:32, one launch (start us, length us, event | category | flops | bytes accessed | tf_op | source)
XLA Modules:
  0.0 573.4 jit_solution(10186639585746647599)
XLA Ops:
  7.2 0.0 copy-start
  7.2 0.0 all-reduce.4.cloned.1.call-start
  7.2 8.4 %copy.13 = f32[2,64,64,128]{1,0,3,2:T(2,128)} copy(f32[2,64,64,128]{3,2,1,0:T(8,128)} %param.5) | data formatting | bytes 8388608 | tf_op args[0]
  15.7 15.1 %reshape.52 = f32[16,1,65536]{2,1,0:T(1,128)} reshape(f32[8192,2,64]{2,1,0:T(2,128)} %bitcast.97) | data formatting | bytes 8388608
  30.8 57.9 %all_to_all.33 = f32[16,1,65536]{2,1,0:T(1,128)} all-to-all(f32[16,1,65536]{2,1,0:T(1,128)} %reshape.52), channel_id=1, replica_groups=mesh['gx'=16,'gy'=2,'gz'=8] {'gx'}, dimensions={0} | all-to-all | bytes 8388608 | tf_op jit(solution)/shard_map/all_to_all | solution.py:18
  88.6 0.5 broadcast.87
  89.1 13.7 %reduce.8 = f32[16,65536]{1,0:T(8,128)} reduce(f32[16,1,65536]{2,1,0:T(1,128)} %all_to_all.33, f32[]{:T(128)} %broadcast.87), dimensions={1}, to_apply=%all_to_all.24.reduce_sub_computation | reduce | bytes 8388612 | tf_op jit(solution)/shard_map/all_to_all | solution.py:18
  102.9 9.7 %reshape.53 = f32[8192,2,64]{2,1,0:T(2,128)} reshape(f32[16,65536]{1,0:T(8,128)} %reduce.8) | data formatting | bytes 8388608
  112.5 12.2 %copy.26 = f32[2,64,16,512]{3,1,2,0:T(8,128)} copy(f32[2,64,16,512]{1,0,3,2:T(2,128)} %bitcast.96) | data formatting | bytes 8388608 | tf_op jit(solution)/shard_map/all_to_all | solution.py:18
  124.7 17.6 %convolution_bitcast_fusion = f32[1024,1024]{1,0:T(8,128)} fusion(f32[2,1024,512]{2,1,0:T(8,128)} %bitcast.98), kind=kOutput, calls=%fused_computation.4 | convolution fusion | flops 12884901888 | bytes 8388608 | tf_op jit(solution)/shard_map/crm,csm->rs/dot_general | solution.py:20
  142.4 0.0 all-reduce.4.cloned.1.call-update
  142.4 0.3 all-reduce.6.cloned.1.call-start
  142.7 118.2 %all-reduce.4.cloned.1.call-done = f32[1024,1024]{1,0:T(8,128)} async-done(((f32[1024,1024]{1,0:T(8,128)}), f32[1024,1024]{1,0:T(8,128)}) %all-reduce.4.cloned.1.call-update) | async-done | bytes 4194320 | tf_op jit(solution)/shard_map/psum | solution.py:21
  260.8 0.0 all-reduce.6.cloned.1.call-update
  260.9 119.8 %all-reduce.6.cloned.1.call-done = f32[1024,1024]{1,0:T(8,128)} async-done(((f32[1024,1024]{1,0:T(8,128)}), f32[1024,1024]{1,0:T(8,128)}) %all-reduce.6.cloned.1.call-update) | async-done | bytes 4194320 | tf_op jit(solution)/shard_map/psum | solution.py:21
  380.7 0.0 copy-done
  380.7 5.2 fusion.32
  385.9 1.8 fusion.33
  387.8 0.1 copy.16
  388.0 11.7 %cholesky.130 = f32[128,128]{1,0:T(8,128)S(1)} custom-call(f32[128,128]{1,0:T(8,128)S(1)} %cholesky.194), custom_call_target="Cholesky" | custom-call | tf_op jit(solution)/shard_map/jit(cholesky)/cholesky | solution.py:11
  399.7 9.8 %custom-call.13 = f32[1,128,128]{1,2,0:T(8,128)S(1)} custom-call(f32[1,128,128]{2,1,0:T(8,128)S(1)} %get-tuple-element.53), custom_call_target="InvertDiagBlocksLowerTriangular" | custom-call | tf_op jit(solution)/shard_map/jit(cholesky)/cholesky | solution.py:11
  409.5 0.2 constant_dynamic-update-slice_fusion.3
  409.8 0.3 convolution_subtract_fusion.3
  410.0 11.7 %cholesky.147 = f32[128,128]{1,0:T(8,128)S(1)} custom-call(f32[128,128]{1,0:T(8,128)S(1)} %convolution_subtract_fusion.3), custom_call_target="Cholesky" | custom-call | tf_op jit(solution)/shard_map/jit(cholesky)/cholesky | solution.py:11
  421.8 0.7 compare_reduce_fusion.2
  436.6 0.1 triangular_solve.75
  436.7 3.9 while.4
  436.7 0.6 fusion.55
  437.3 1.4 bitcast_dynamic-update-slice_fusion.4
  438.7 0.6 fusion.55
  439.2 1.4 bitcast_dynamic-update-slice_fusion.4
  440.6 19.7 %custom-call.14 = f32[2,128,128]{1,2,0:T(8,128)S(1)} custom-call(f32[2,128,128]{2,1,0:T(8,128)S(1)} %get-tuple-element.18), custom_call_target="InvertDiagBlocksLowerTriangular" | custom-call | tf_op jit(solution)/shard_map/jit(_solve_triangular)/triangular_solve | solution.py:12
  460.3 0.6 fusion.8
  460.9 1.0 convolution_subtract_fusion.1
  461.9 0.6 fusion.19
  462.6 5.3 fusion.2
  467.9 1.8 fusion.34
  469.8 0.1 copy.18
  470.0 11.7 %cholesky.164 = f32[128,128]{1,0:T(8,128)S(1)} custom-call(f32[128,128]{1,0:T(8,128)S(1)} %cholesky.197), custom_call_target="Cholesky" | custom-call | tf_op jit(solution)/shard_map/jit(cholesky)/cholesky | solution.py:11
  481.7 9.8 %custom-call.15 = f32[1,128,128]{1,2,0:T(8,128)S(1)} custom-call(f32[1,128,128]{2,1,0:T(8,128)S(1)} %get-tuple-element.49), custom_call_target="InvertDiagBlocksLowerTriangular" | custom-call | tf_op jit(solution)/shard_map/jit(cholesky)/cholesky | solution.py:11
  491.6 0.2 constant_dynamic-update-slice_fusion.1
  491.8 0.3 convolution_subtract_fusion.2
  492.0 11.7 %cholesky.181 = f32[128,128]{1,0:T(8,128)S(1)} custom-call(f32[128,128]{1,0:T(8,128)S(1)} %convolution_subtract_fusion.2), custom_call_target="Cholesky" | custom-call | tf_op jit(solution)/shard_map/jit(cholesky)/cholesky | solution.py:11
  503.8 0.6 compare_reduce_fusion
  504.4 0.6 compare_reduce_fusion.1
  506.4 0.2 select_select_fusion
  506.6 4.0 while.5
  506.7 0.6 fusion.56
  507.2 1.4 bitcast_dynamic-update-slice_fusion.5
  508.7 0.6 fusion.56
  509.2 1.4 bitcast_dynamic-update-slice_fusion.5
  510.6 19.7 %custom-call.16 = f32[2,128,128]{1,2,0:T(8,128)S(1)} custom-call(f32[2,128,128]{2,1,0:T(8,128)S(1)} %get-tuple-element.19), custom_call_target="InvertDiagBlocksLowerTriangular" | custom-call | tf_op jit(solution)/shard_map/jit(_solve_triangular)/triangular_solve | solution.py:12
  530.3 0.6 fusion.6
  531.0 1.0 convolution_subtract_fusion
  532.0 0.6 fusion.15
  532.6 5.7 convolution_bitcast_fusion.1
  538.3 1.8 copy.20
  540.1 5.4 all-to-all-start.1
  545.5 0.1 fusion.13
  545.6 0.7 copy.22
  546.3 16.9 %all-to-all-done.1 = f32[2,256,512]{2,0,1:T(2,128)} async-done(((f32[2,256,512]{2,0,1:T(2,128)}), f32[2,256,512]{2,0,1:T(2,128)}, u32[]{:S(2)}, u32[]{:S(2)}) %all-to-all-start.1) | async-done | bytes 1048608 | tf_op jit(solution)/shard_map/all_to_all | solution.py:26
  563.3 1.8 copy.21
  565.1 1.0 reshape.27
  (18 shorter events, 0.4 us)
Async XLA Ops:
  7.2 373.5 %copy-start = (f32[1024,256]{1,0:T(8,128)S(1)}, f32[1024,256]{1,0:T(8,128)}, u32[]{:S(2)}) copy-start(f32[1024,256]{1,0:T(8,128)} %param.6) | copy-start | bytes 3145732
  7.2 253.7 %all-reduce.4.cloned.1.call-start = ((), (), s32[]{:S(2)}) async-start(), calls=%async_computation.2 | async-start | bytes 8388608 | tf_op jit(solution)/shard_map/psum | solution.py:21
  142.4 238.3 %all-reduce.6.cloned.1.call-start = ((), (), s32[]{:S(2)}) async-start(), calls=%async_computation.3 | async-start | bytes 8388608 | tf_op jit(solution)/shard_map/psum | solution.py:21
  540.1 23.1 %all-to-all-start.1 = ((f32[2,256,512]{2,0,1:T(2,128)}), f32[2,256,512]{2,0,1:T(2,128)}, u32[]{:S(2)}, u32[]{:S(2)}) async-start(f32[2,256,512]{2,0,1:T(2,128)} %copy.20), calls=%async_computation.1 | async-start | bytes 2097152 | tf_op jit(solution)/shard_map/all_to_all | solution.py:26
Sparse Core Ops, SparseCore 0:
  142.5 118.3 all-reduce.3
  264.2 116.4 all-reduce.5
